TPU v7x, 512 devices: a whole 4x8x8 slice. The times are simulated.
512 devices in a mesh: group: 8 (over y), mesh: 32 (over z, x), comp: 2 (over core).
Axes of the slice: x: 4, y: 8, z: 8, core: 2. Of those that a mesh axis runs over, the one named last changes fastest.
Arguments:
- log_sigma: float32 [2048, 128], P('mesh'), may hold values from -1 to 1
- block_owner: int32 [8, 4096, 1], P('group', 'mesh'), may hold values from 0 to 31; in each aligned block of 128 rows (0 to 127, 128 to 255, ..., all dimensions but the last counted through in order) at most 8 rows name the same one
- block_slot: int32 [8, 4096], P('group', 'mesh'), may hold values from 0 to 63
- coupling: float32 [128, 128], replicated, may hold values from -0.6 to 10, as said below
- sources: float32 [8, 2, 8, 4096, 128], P('group', 'comp', None, 'mesh'), may hold values from -24 to 24
- rcv_cell: int32 [8, 4096], P('group', 'mesh'), may hold values from 0 to 16383
- observed: float32 [8, 2, 8, 4096], P('group', 'comp', None, 'mesh'), may hold values from -6 to 6
Outputs:
- gradient: float32 [2048, 128], P('mesh')
Inputs may be any that keep to these rules, and one draw needn't show every extreme that they name: `block_owner`: in the 128 rows of one device of a group, no owner is named more than 8 times; some owner is named exactly 8 times in some device's rows. `rcv_cell`: A receiver's cell counts from the first cell of the modelling section of the device that holds the receiver's entry. `coupling`: every diagonal entry is 6 or more.
All inputs are finite; a program needn't handle non-finite values.
Results may differ from a plain program's by a relative error of at most 0.0003.
Values sent between devices are 32-bit elements; how exact they have to be, the bound alone decides.
A program may use at most 64 MiB of HBM per device.

v0:
```python
import jax
import jax.numpy as jnp
from jax import lax
from jax.sharding import PartitionSpec as P

CELLS = 128
S = 8
ITERS = 6
omega_freq = 0.8
chain_weight = 1.0


def from_partner(value, axis, distance):
    mask = 2**distance
    pairs = [(source, source ^ mask) for source in range(lax.axis_size(axis))]
    return lax.ppermute(value, axis, pairs)


def with_halo(x, sides, width):
    for axis, dim in sides:
        size, length = (lax.axis_size(axis), x.shape[dim])
        up = [(i, (i + 1) % size) for i in range(size - 1)]
        down = [(j, i) for i, j in up]
        last = lax.slice_in_dim(x, length - width, length, axis=dim)
        initial = lax.slice_in_dim(x, 0, width, axis=dim)
        before = lax.ppermute(last, axis, up)
        after = lax.ppermute(initial, axis, down)
        x = jnp.concatenate([before, x, after], axis=dim)
    return x


def partner(values):
    return from_partner(values, "comp", 0)


def beside(values):
    padded = with_halo(values, (("mesh", 1),), 1)
    return padded[:, :-2] + padded[:, 2:]


def cell_product(values, matrix):
    shaped = values.reshape(values.shape[:-1] + (-1, CELLS))
    product = jnp.einsum("...bj,ij->...bi", shaped, matrix, precision=lax.Precision.HIGHEST)
    return product.reshape(values.shape)


def operate(values, matrix, cross_coef):
    return (
        cell_product(values, matrix) - chain_weight * beside(values) + cross_coef * partner(values)
    )


def relax(right, matrix, cross_coef, inverse_diag, apply_op):
    state = jnp.zeros_like(right)
    for iteration in range(ITERS):
        state = state + inverse_diag * (right - apply_op(state, matrix, cross_coef))
    return state


def local(log_sigma, block_owner, block_slot, coupling, sources, rcv_cell, observed):
    owners = block_owner[0, :, 0]
    slots = block_slot[0]
    blocks_dev = owners.shape[0]
    inv_rows = log_sigma.shape[0]
    targets = owners * inv_rows + slots
    gathered = lax.all_gather(log_sigma, "mesh", axis=0, tiled=True)
    model_part = jnp.take(gathered, targets, axis=0)
    sigmas = jnp.exp(model_part).reshape(-1)
    receivers = rcv_cell[0]
    parity = (2 * lax.axis_index("comp") - 1).astype(jnp.float32)
    forward_coef = parity * omega_freq * sigmas
    inverse_diag = jnp.tile(1.0 / jnp.diagonal(coupling), blocks_dev)
    right = sources.reshape(S, -1)
    field_now = relax(right, coupling, forward_coef, inverse_diag, operate)
    field_other = partner(field_now)
    misfit = field_now[:, receivers] - observed[0, 0]
    adjoint_src = jnp.zeros_like(right).at[:, receivers].add(misfit)
    adjoint = relax(adjoint_src, coupling.T, -forward_coef, inverse_diag, operate)
    weighted = -parity * jnp.sum(adjoint * field_other, axis=0)
    partial_rows = (omega_freq * sigmas * weighted).reshape(blocks_dev, CELLS)
    inside_rows = (targets >= 0) & (targets < inv_rows * lax.axis_size("mesh"))
    kept_rows = jnp.where(inside_rows, targets, inv_rows * lax.axis_size("mesh"))
    owned = lax.psum_scatter(
        jnp.zeros((inv_rows * lax.axis_size("mesh"), CELLS), jnp.float32)
        .at[kept_rows]
        .add(partial_rows, mode="drop"),
        "mesh",
        scatter_dimension=0,
        tiled=True,
    )
    return lax.psum(owned, ("group", "comp"))


def solution(mesh):
    in_specs = (
        P("mesh", None),
        P("group", "mesh", None),
        P("group", "mesh"),
        P(),
        P("group", "comp", None, "mesh", None),
        P("group", "mesh"),
        P("group", "comp", None, "mesh"),
    )
    out_specs = P("mesh", None)
    return jax.shard_map(local, mesh=mesh, in_specs=in_specs, out_specs=out_specs, check_vma=False)
```

profile of v0, /device:TPU:32, one launch (start us, length us, event | category | flops | bytes accessed | tf_op | source)
XLA Modules:
  0.0 532.8 jit_solution(2460921501740615536)
XLA Ops:
  7.3 1.3 collective-permute-start.1
  8.6 4.5 collective-permute-start
  13.2 1.9 collective-permute-start.2
  18.4 78.7 %all-gather.2.cloned.1.call-done = f32[2048,128]{1,0:T(8,128)} async-done(((f32[64,128]{1,0:T(8,128)}), f32[2048,128]{1,0:T(8,128)}) %all-gather.2.cloned.1.call-update) | async-done | bytes 1048592 | tf_op jit(solution)/shard_map/all_gather | solution.py:66
  97.1 1.9 gather_fusion
  99.1 1.7 fusion.8
  100.8 1.9 collective-permute-start.5
  102.8 1.3 collective-permute-start.4
  104.1 4.5 collective-permute-start.3
  108.6 1.3 collective-permute-done.3
  109.9 1.9 fusion.10
  111.9 1.9 collective-permute-start.8
  113.9 1.3 collective-permute-start.7
  115.2 4.8 collective-permute-start.6
  121.8 1.9 collective-permute-start.11
  123.8 1.3 collective-permute-start.10
  125.1 4.8 collective-permute-start.9
  129.9 1.3 collective-permute-done.9
  132.1 1.9 collective-permute-start.14
  134.1 1.3 collective-permute-start.13
  135.4 4.8 collective-permute-start.12
  142.1 1.9 collective-permute-start.17
  144.8 1.3 collective-permute-start.16
  146.1 5.5 %collective-permute-start.15 = (f32[8,1]{1,0:T(8,128)S(1)}, f32[8,1]{1,0:T(8,128)S(1)}, u32[]{:S(2)}, u32[]{:S(2)}) collective-permute-start(f32[8,1]{1,0:T(8,128)S(1)} %get-tuple-element.17), channel_id=1, source_target_pairs={{0,2},{2,4},{4,6},{6,8},{8,10},{10,12},{12,14},{14,16},{16,18},{18... | collective-permute-start | bytes 104 | tf_op jit(solution)/shard_map/ppermute | solution.py:26
  151.6 1.3 collective-permute-done.15
  152.9 1.9 fusion.18
  154.8 5.3 copy.271
  160.1 6.0 %scatter_custom_fusion = f32[8,16384]{0,1:T(8,128)} fusion(s32[128]{0:T(128)S(1)} %fusion.122, f32[]{:T(128)} %constant.12.clone.1, f32[1,1,8,128]{2,3,1,0:T(8,128)S(1)} %copy.272, f32[8,16384]{0,1:T(8,128)} %copy.271, s32[1024]{0:T(1024)S(1)} %pad_clamp_fusion), kind=kCustom, calls=%fused_computation.15 | custom fusion | flops 2048 | bytes 1118212 | tf_op jit(solution)/shard_map/scatter-add | solution.py:77
  166.1 5.5 %copy.273 = f32[8,16384]{1,0:T(8,128)S(1)} copy(f32[8,16384]{0,1:T(8,128)} %scatter_custom_fusion) | data formatting | bytes 1048576 | tf_op jit(solution)/shard_map/scatter-add | solution.py:77
  172.0 1.9 collective-permute-start.20
  174.0 1.3 collective-permute-start.19
  175.3 6.9 %collective-permute-start.18 = (f32[8,1]{1,0:T(8,128)S(1)}, f32[8,1]{1,0:T(8,128)S(1)}, u32[]{:S(2)}, u32[]{:S(2)}) collective-permute-start(f32[8,1]{1,0:T(8,128)S(1)} %get-tuple-element.15), channel_id=1, source_target_pairs={{0,2},{2,4},{4,6},{6,8},{8,10},{10,12},{12,14},{14,16},{16,18},{18... | collective-permute-start | bytes 104 | tf_op jit(solution)/shard_map/ppermute | solution.py:26
  182.3 1.3 collective-permute-done.18
  184.2 1.9 collective-permute-start.23
  186.2 1.3 collective-permute-start.22
  187.5 6.9 %collective-permute-start.21 = (f32[8,1]{1,0:T(8,128)S(1)}, f32[8,1]{1,0:T(8,128)S(1)}, u32[]{:S(2)}, u32[]{:S(2)}) collective-permute-start(f32[8,1]{1,0:T(8,128)S(1)} %get-tuple-element.13), channel_id=1, source_target_pairs={{0,2},{2,4},{4,6},{6,8},{8,10},{10,12},{12,14},{14,16},{16,18},{18... | collective-permute-start | bytes 104 | tf_op jit(solution)/shard_map/ppermute | solution.py:26
  196.2 1.9 collective-permute-start.26
  199.5 6.9 %collective-permute-start.24 = (f32[8,1]{1,0:T(8,128)S(1)}, f32[8,1]{1,0:T(8,128)S(1)}, u32[]{:S(2)}, u32[]{:S(2)}) collective-permute-start(f32[8,1]{1,0:T(8,128)S(1)} %get-tuple-element.11), channel_id=1, source_target_pairs={{0,2},{2,4},{4,6},{6,8},{8,10},{10,12},{12,14},{14,16},{16,18},{18... | collective-permute-start | bytes 104 | tf_op jit(solution)/shard_map/ppermute | solution.py:26
  206.4 1.3 collective-permute-done.24
  208.4 1.9 collective-permute-start.29
  210.3 2.4 collective-permute-start.33
  214.1 6.9 %collective-permute-start.27 = (f32[8,1]{1,0:T(8,128)S(1)}, f32[8,1]{1,0:T(8,128)S(1)}, u32[]{:S(2)}, u32[]{:S(2)}) collective-permute-start(f32[8,1]{1,0:T(8,128)S(1)} %get-tuple-element.9), channel_id=1, source_target_pairs={{0,2},{2,4},{4,6},{6,8},{8,10},{10,12},{12,14},{14,16},{16,18},{18... | collective-permute-start | bytes 104 | tf_op jit(solution)/shard_map/ppermute | solution.py:26
  222.8 1.9 collective-permute-start.32
  224.8 1.3 collective-permute-start.31
  226.1 6.9 %collective-permute-start.30 = (f32[8,1]{1,0:T(8,128)S(1)}, f32[8,1]{1,0:T(8,128)S(1)}, u32[]{:S(2)}, u32[]{:S(2)}) collective-permute-start(f32[8,1]{1,0:T(8,128)S(1)} %get-tuple-element.7), channel_id=1, source_target_pairs={{0,2},{2,4},{4,6},{6,8},{8,10},{10,12},{12,14},{14,16},{16,18},{18... | collective-permute-start | bytes 104 | tf_op jit(solution)/shard_map/ppermute | solution.py:26
  234.7 2.1 scatter_custom_fusion.1
  236.8 242.3 %reduce-scatter.2.cloned.1.call-done = f32[64,128]{1,0:T(8,128)} async-done(((f32[2048,128]{1,0:T(8,128)}), f32[64,128]{1,0:T(8,128)}) %reduce-scatter.2.cloned.1.call-update) | async-done | bytes 32784 | tf_op jit(solution)/shard_map/reduce_scatter | solution.py:83
  479.1 46.9 %psum.7 = f32[64,128]{1,0:T(8,128)} all-reduce(f32[64,128]{1,0:T(8,128)} %reduce-scatter.2.cloned.1.call-done), channel_id=1, replica_groups=mesh['group'=8,'mesh'=32,'comp'=2] {'group','comp'}, use_global_device_ids=true, to_apply=%region_4.5 | all-reduce | flops 8192 | bytes 65536 | tf_op jit(solution)/shard_map/psum | solution.py:91
  (82 shorter events, 19.5 us)
Async XLA Ops:
  6.5 8.7 %copy-start = (f32[128,128]{1,0:T(8,128)S(1)}, f32[128,128]{1,0:T(8,128)}, u32[]{:S(2)}) copy-start(f32[128,128]{1,0:T(8,128)} %param.10) | copy-start | bytes 196612
  6.5 114.8 %copy-start.1 = (f32[1,1,8,128,128]{4,3,2,1,0:T(8,128)S(1)}, f32[1,1,8,128,128]{4,3,2,1,0:T(8,128)}, u32[]{:S(2)}) copy-start(f32[1,1,8,128,128]{4,3,2,1,0:T(8,128)} %param.11) | copy-start | bytes 1572868
  6.5 90.6 %all-gather.2.cloned.1.call-start = ((), (), s32[]{:S(2)}) async-start(), calls=%async_computation.1 | async-start | bytes 1081344 | tf_op jit(solution)/shard_map/all_gather | solution.py:66
  7.3 471.8 %reduce-scatter.2.cloned.1.call-start = ((), (), s32[]{:S(2)}) async-start(), calls=%async_computation.2 | async-start | bytes 1081344 | tf_op jit(solution)/shard_map/reduce_scatter | solution.py:83
  7.3 91.8 %collective-permute-start.1 = (f32[8,1]{1,0:T(8,128)S(1)}, f32[8,1]{1,0:T(8,128)S(1)}, u32[]{:S(2)}, u32[]{:S(2)}) collective-permute-start(f32[8,1]{1,0:T(8,128)S(1)} %broadcast.157), channel_id=1, source_target_pairs={{2,0},{4,2},{6,4},{8,6},{10,8},{12,10},{14,12},{16,14},{18,16},{20... | collective-permute-start | bytes 104 | tf_op jit(solution)/shard_map/ppermute | solution.py:27
  8.6 90.5 %collective-permute-start = (f32[8,1]{1,0:T(8,128)S(1)}, f32[8,1]{1,0:T(8,128)S(1)}, u32[]{:S(2)}, u32[]{:S(2)}) collective-permute-start(f32[8,1]{1,0:T(8,128)S(1)} %broadcast.157), channel_id=1, source_target_pairs={{0,2},{2,4},{4,6},{6,8},{8,10},{10,12},{12,14},{14,16},{16,18},{18... | collective-permute-start | bytes 104 | tf_op jit(solution)/shard_map/ppermute | solution.py:26
  13.2 130.8 %copy-start.3 = (s32[1,128]{1,0:T(1,128)S(1)}, s32[1,128]{1,0:T(1,128)}, u32[]{:S(2)}) copy-start(s32[1,128]{1,0:T(1,128)} %param.12) | copy-start | bytes 1540
  13.2 130.8 %copy-start.2 = (f32[1,1,8,128]{3,2,1,0:T(8,128)S(1)}, f32[1,1,8,128]{3,2,1,0:T(8,128)}, u32[]{:S(2)}) copy-start(f32[1,1,8,128]{3,2,1,0:T(8,128)} %param.13) | copy-start | bytes 12292
  13.2 85.8 %collective-permute-start.2 = (f32[8,16384]{1,0:T(8,128)S(1)}, f32[8,16384]{1,0:T(8,128)S(1)}, u32[]{:S(2)}, u32[]{:S(2)}) collective-permute-start(f32[8,16384]{1,0:T(8,128)S(1)} %broadcast.154.clone), channel_id=1, source_target_pairs={{0,1},{1,0},{2,3},{3,2},{4,5},{5,4},{6,7},{7,6},{8,9},{9,8},{10,11... | collective-permute-start | bytes 1572872 | tf_op jit(solution)/shard_map/ppermute | solution.py:16
  100.8 9.2 %collective-permute-start.5 = (f32[8,16384]{1,0:T(8,128)S(1)}, f32[8,16384]{1,0:T(8,128)S(1)}, u32[]{:S(2)}, u32[]{:S(2)}) collective-permute-start(f32[8,16384]{1,0:T(8,128)S(1)} %fusion.8), channel_id=1, source_target_pairs={{0,1},{1,0},{2,3},{3,2},{4,5},{5,4},{6,7},{7,6},{8,9},{9,8},{10,11... | collective-permute-start | bytes 1572872 | tf_op jit(solution)/shard_map/ppermute | solution.py:16
  102.8 5.8 %collective-permute-start.4 = (f32[8,1]{1,0:T(8,128)S(1)}, f32[8,1]{1,0:T(8,128)S(1)}, u32[]{:S(2)}, u32[]{:S(2)}) collective-permute-start(f32[8,1]{1,0:T(8,128)S(1)} %get-tuple-element.26), channel_id=1, source_target_pairs={{2,0},{4,2},{6,4},{8,6},{10,8},{12,10},{14,12},{16,14},{18,16},{20... | collective-permute-start | bytes 104 | tf_op jit(solution)/shard_map/ppermute | solution.py:27
  104.1 5.9 %collective-permute-start.3 = (f32[8,1]{1,0:T(8,128)S(1)}, f32[8,1]{1,0:T(8,128)S(1)}, u32[]{:S(2)}, u32[]{:S(2)}) collective-permute-start(f32[8,1]{1,0:T(8,128)S(1)} %get-tuple-element.25), channel_id=1, source_target_pairs={{0,2},{2,4},{4,6},{6,8},{8,10},{10,12},{12,14},{14,16},{16,18},{18... | collective-permute-start | bytes 104 | tf_op jit(solution)/shard_map/ppermute | solution.py:26
  111.9 9.4 %collective-permute-start.8 = (f32[8,16384]{1,0:T(8,128)S(1)}, f32[8,16384]{1,0:T(8,128)S(1)}, u32[]{:S(2)}, u32[]{:S(2)}) collective-permute-start(f32[8,16384]{1,0:T(8,128)S(1)} %fusion.10), channel_id=1, source_target_pairs={{0,1},{1,0},{2,3},{3,2},{4,5},{5,4},{6,7},{7,6},{8,9},{9,8},{10,11... | collective-permute-start | bytes 1572872 | tf_op jit(solution)/shard_map/ppermute | solution.py:16
  113.9 6.7 %collective-permute-start.7 = (f32[8,1]{1,0:T(8,128)S(1)}, f32[8,1]{1,0:T(8,128)S(1)}, u32[]{:S(2)}, u32[]{:S(2)}) collective-permute-start(f32[8,1]{1,0:T(8,128)S(1)} %get-tuple-element.24), channel_id=1, source_target_pairs={{2,0},{4,2},{6,4},{8,6},{10,8},{12,10},{14,12},{16,14},{18,16},{20... | collective-permute-start | bytes 104 | tf_op jit(solution)/shard_map/ppermute | solution.py:27
  115.2 6.1 %collective-permute-start.6 = (f32[8,1]{1,0:T(8,128)S(1)}, f32[8,1]{1,0:T(8,128)S(1)}, u32[]{:S(2)}, u32[]{:S(2)}) collective-permute-start(f32[8,1]{1,0:T(8,128)S(1)} %get-tuple-element.23), channel_id=1, source_target_pairs={{0,2},{2,4},{4,6},{6,8},{8,10},{10,12},{12,14},{14,16},{16,18},{18... | collective-permute-start | bytes 104 | tf_op jit(solution)/shard_map/ppermute | solution.py:26
  121.8 9.4 %collective-permute-start.11 = (f32[8,16384]{1,0:T(8,128)S(1)}, f32[8,16384]{1,0:T(8,128)S(1)}, u32[]{:S(2)}, u32[]{:S(2)}) collective-permute-start(f32[8,16384]{1,0:T(8,128)S(1)} %fusion.12), channel_id=1, source_target_pairs={{0,1},{1,0},{2,3},{3,2},{4,5},{5,4},{6,7},{7,6},{8,9},{9,8},{10,11... | collective-permute-start | bytes 1572872 | tf_op jit(solution)/shard_map/ppermute | solution.py:16
  123.8 6.1 %collective-permute-start.10 = (f32[8,1]{1,0:T(8,128)S(1)}, f32[8,1]{1,0:T(8,128)S(1)}, u32[]{:S(2)}, u32[]{:S(2)}) collective-permute-start(f32[8,1]{1,0:T(8,128)S(1)} %get-tuple-element.22), channel_id=1, source_target_pairs={{2,0},{4,2},{6,4},{8,6},{10,8},{12,10},{14,12},{16,14},{18,16},{20... | collective-permute-start | bytes 104 | tf_op jit(solution)/shard_map/ppermute | solution.py:27
  125.1 6.1 %collective-permute-start.9 = (f32[8,1]{1,0:T(8,128)S(1)}, f32[8,1]{1,0:T(8,128)S(1)}, u32[]{:S(2)}, u32[]{:S(2)}) collective-permute-start(f32[8,1]{1,0:T(8,128)S(1)} %get-tuple-element.21), channel_id=1, source_target_pairs={{0,2},{2,4},{4,6},{6,8},{8,10},{10,12},{12,14},{14,16},{16,18},{18... | collective-permute-start | bytes 104 | tf_op jit(solution)/shard_map/ppermute | solution.py:26
  132.1 9.4 %collective-permute-start.14 = (f32[8,16384]{1,0:T(8,128)S(1)}, f32[8,16384]{1,0:T(8,128)S(1)}, u32[]{:S(2)}, u32[]{:S(2)}) collective-permute-start(f32[8,16384]{1,0:T(8,128)S(1)} %fusion.14), channel_id=1, source_target_pairs={{0,1},{1,0},{2,3},{3,2},{4,5},{5,4},{6,7},{7,6},{8,9},{9,8},{10,11... | collective-permute-start | bytes 1572872 | tf_op jit(solution)/shard_map/ppermute | solution.py:16
  134.1 6.7 %collective-permute-start.13 = (f32[8,1]{1,0:T(8,128)S(1)}, f32[8,1]{1,0:T(8,128)S(1)}, u32[]{:S(2)}, u32[]{:S(2)}) collective-permute-start(f32[8,1]{1,0:T(8,128)S(1)} %get-tuple-element.20), channel_id=1, source_target_pairs={{2,0},{4,2},{6,4},{8,6},{10,8},{12,10},{14,12},{16,14},{18,16},{20... | collective-permute-start | bytes 104 | tf_op jit(solution)/shard_map/ppermute | solution.py:27
  135.4 6.1 %collective-permute-start.12 = (f32[8,1]{1,0:T(8,128)S(1)}, f32[8,1]{1,0:T(8,128)S(1)}, u32[]{:S(2)}, u32[]{:S(2)}) collective-permute-start(f32[8,1]{1,0:T(8,128)S(1)} %get-tuple-element.19), channel_id=1, source_target_pairs={{0,2},{2,4},{4,6},{6,8},{8,10},{10,12},{12,14},{14,16},{16,18},{18... | collective-permute-start | bytes 104 | tf_op jit(solution)/shard_map/ppermute | solution.py:26
  142.1 10.8 %collective-permute-start.17 = (f32[8,16384]{1,0:T(8,128)S(1)}, f32[8,16384]{1,0:T(8,128)}, u32[]{:S(2)}, u32[]{:S(2)}) collective-permute-start(f32[8,16384]{1,0:T(8,128)S(1)} %fusion.16), channel_id=1, source_target_pairs={{0,1},{1,0},{2,3},{3,2},{4,5},{5,4},{6,7},{7,6},{8,9},{9,8},{10,11... | collective-permute-start | bytes 1572872 | tf_op jit(solution)/shard_map/ppermute | solution.py:16
  144.8 6.8 %collective-permute-start.16 = (f32[8,1]{1,0:T(8,128)S(1)}, f32[8,1]{1,0:T(8,128)S(1)}, u32[]{:S(2)}, u32[]{:S(2)}) collective-permute-start(f32[8,1]{1,0:T(8,128)S(1)} %get-tuple-element.18), channel_id=1, source_target_pairs={{2,0},{4,2},{6,4},{8,6},{10,8},{12,10},{14,12},{16,14},{18,16},{20... | collective-permute-start | bytes 104 | tf_op jit(solution)/shard_map/ppermute | solution.py:27
  146.1 6.8 %collective-permute-start.15 = (f32[8,1]{1,0:T(8,128)S(1)}, f32[8,1]{1,0:T(8,128)S(1)}, u32[]{:S(2)}, u32[]{:S(2)}) collective-permute-start(f32[8,1]{1,0:T(8,128)S(1)} %get-tuple-element.17), channel_id=1, source_target_pairs={{0,2},{2,4},{4,6},{6,8},{8,10},{10,12},{12,14},{14,16},{16,18},{18... | collective-permute-start | bytes 104 | tf_op jit(solution)/shard_map/ppermute | solution.py:26
  172.0 11.5 %collective-permute-start.20 = (f32[8,16384]{1,0:T(8,128)S(1)}, f32[8,16384]{1,0:T(8,128)S(1)}, u32[]{:S(2)}, u32[]{:S(2)}) collective-permute-start(f32[8,16384]{1,0:T(8,128)S(1)} %fusion.5), channel_id=1, source_target_pairs={{0,1},{1,0},{2,3},{3,2},{4,5},{5,4},{6,7},{7,6},{8,9},{9,8},{10,11... | collective-permute-start | bytes 1572872 | tf_op jit(solution)/shard_map/ppermute | solution.py:16
  174.0 8.2 %collective-permute-start.19 = (f32[8,1]{1,0:T(8,128)S(1)}, f32[8,1]{1,0:T(8,128)S(1)}, u32[]{:S(2)}, u32[]{:S(2)}) collective-permute-start(f32[8,1]{1,0:T(8,128)S(1)} %get-tuple-element.16), channel_id=1, source_target_pairs={{2,0},{4,2},{6,4},{8,6},{10,8},{12,10},{14,12},{16,14},{18,16},{20... | collective-permute-start | bytes 104 | tf_op jit(solution)/shard_map/ppermute | solution.py:27
  175.3 8.3 %collective-permute-start.18 = (f32[8,1]{1,0:T(8,128)S(1)}, f32[8,1]{1,0:T(8,128)S(1)}, u32[]{:S(2)}, u32[]{:S(2)}) collective-permute-start(f32[8,1]{1,0:T(8,128)S(1)} %get-tuple-element.15), channel_id=1, source_target_pairs={{0,2},{2,4},{4,6},{6,8},{8,10},{10,12},{12,14},{14,16},{16,18},{18... | collective-permute-start | bytes 104 | tf_op jit(solution)/shard_map/ppermute | solution.py:26
  184.2 11.5 %collective-permute-start.23 = (f32[8,16384]{1,0:T(8,128)S(1)}, f32[8,16384]{1,0:T(8,128)S(1)}, u32[]{:S(2)}, u32[]{:S(2)}) collective-permute-start(f32[8,16384]{1,0:T(8,128)S(1)} %fusion.50), channel_id=1, source_target_pairs={{0,1},{1,0},{2,3},{3,2},{4,5},{5,4},{6,7},{7,6},{8,9},{9,8},{10,11... | collective-permute-start | bytes 1572872 | tf_op jit(solution)/shard_map/ppermute | solution.py:16
  186.2 8.8 %collective-permute-start.22 = (f32[8,1]{1,0:T(8,128)S(1)}, f32[8,1]{1,0:T(8,128)S(1)}, u32[]{:S(2)}, u32[]{:S(2)}) collective-permute-start(f32[8,1]{1,0:T(8,128)S(1)} %get-tuple-element.14), channel_id=1, source_target_pairs={{2,0},{4,2},{6,4},{8,6},{10,8},{12,10},{14,12},{16,14},{18,16},{20... | collective-permute-start | bytes 104 | tf_op jit(solution)/shard_map/ppermute | solution.py:27
  187.5 8.2 %collective-permute-start.21 = (f32[8,1]{1,0:T(8,128)S(1)}, f32[8,1]{1,0:T(8,128)S(1)}, u32[]{:S(2)}, u32[]{:S(2)}) collective-permute-start(f32[8,1]{1,0:T(8,128)S(1)} %get-tuple-element.13), channel_id=1, source_target_pairs={{0,2},{2,4},{4,6},{6,8},{8,10},{10,12},{12,14},{14,16},{16,18},{18... | collective-permute-start | bytes 104 | tf_op jit(solution)/shard_map/ppermute | solution.py:26
  196.2 11.5 %collective-permute-start.26 = (f32[8,16384]{1,0:T(8,128)S(1)}, f32[8,16384]{1,0:T(8,128)S(1)}, u32[]{:S(2)}, u32[]{:S(2)}) collective-permute-start(f32[8,16384]{1,0:T(8,128)S(1)} %fusion.44), channel_id=1, source_target_pairs={{0,1},{1,0},{2,3},{3,2},{4,5},{5,4},{6,7},{7,6},{8,9},{9,8},{10,11... | collective-permute-start | bytes 1572872 | tf_op jit(solution)/shard_map/ppermute | solution.py:16
  198.2 8.2 %collective-permute-start.25 = (f32[8,1]{1,0:T(8,128)S(1)}, f32[8,1]{1,0:T(8,128)S(1)}, u32[]{:S(2)}, u32[]{:S(2)}) collective-permute-start(f32[8,1]{1,0:T(8,128)S(1)} %get-tuple-element.12), channel_id=1, source_target_pairs={{2,0},{4,2},{6,4},{8,6},{10,8},{12,10},{14,12},{16,14},{18,16},{20... | collective-permute-start | bytes 104 | tf_op jit(solution)/shard_map/ppermute | solution.py:27
  199.5 8.2 %collective-permute-start.24 = (f32[8,1]{1,0:T(8,128)S(1)}, f32[8,1]{1,0:T(8,128)S(1)}, u32[]{:S(2)}, u32[]{:S(2)}) collective-permute-start(f32[8,1]{1,0:T(8,128)S(1)} %get-tuple-element.11), channel_id=1, source_target_pairs={{0,2},{2,4},{4,6},{6,8},{8,10},{10,12},{12,14},{14,16},{16,18},{18... | collective-permute-start | bytes 104 | tf_op jit(solution)/shard_map/ppermute | solution.py:26
  208.4 14.0 %collective-permute-start.29 = (f32[8,16384]{1,0:T(8,128)S(1)}, f32[8,16384]{1,0:T(8,128)S(1)}, u32[]{:S(2)}, u32[]{:S(2)}) collective-permute-start(f32[8,16384]{1,0:T(8,128)S(1)} %fusion.38), channel_id=1, source_target_pairs={{0,1},{1,0},{2,3},{3,2},{4,5},{5,4},{6,7},{7,6},{8,9},{9,8},{10,11... | collective-permute-start | bytes 1572872 | tf_op jit(solution)/shard_map/ppermute | solution.py:16
  210.3 23.2 %collective-permute-start.33 = (f32[8,16384]{1,0:T(8,128)S(1)}, f32[8,16384]{1,0:T(8,128)S(1)}, u32[]{:S(2)}, u32[]{:S(2)}) collective-permute-start(f32[8,16384]{1,0:T(8,128)S(1)} %fusion.18), channel_id=1, source_target_pairs={{0,1},{1,0},{2,3},{3,2},{4,5},{5,4},{6,7},{7,6},{8,9},{9,8},{10,11... | collective-permute-start | bytes 1572872 | tf_op jit(solution)/shard_map/ppermute | solution.py:16
  212.8 8.8 %collective-permute-start.28 = (f32[8,1]{1,0:T(8,128)S(1)}, f32[8,1]{1,0:T(8,128)S(1)}, u32[]{:S(2)}, u32[]{:S(2)}) collective-permute-start(f32[8,1]{1,0:T(8,128)S(1)} %get-tuple-element.10), channel_id=1, source_target_pairs={{2,0},{4,2},{6,4},{8,6},{10,8},{12,10},{14,12},{16,14},{18,16},{20... | collective-permute-start | bytes 104 | tf_op jit(solution)/shard_map/ppermute | solution.py:27
  214.1 8.3 %collective-permute-start.27 = (f32[8,1]{1,0:T(8,128)S(1)}, f32[8,1]{1,0:T(8,128)S(1)}, u32[]{:S(2)}, u32[]{:S(2)}) collective-permute-start(f32[8,1]{1,0:T(8,128)S(1)} %get-tuple-element.9), channel_id=1, source_target_pairs={{0,2},{2,4},{4,6},{6,8},{8,10},{10,12},{12,14},{14,16},{16,18},{18... | collective-permute-start | bytes 104 | tf_op jit(solution)/shard_map/ppermute | solution.py:26
  222.8 11.5 %collective-permute-start.32 = (f32[8,16384]{1,0:T(8,128)S(1)}, f32[8,16384]{1,0:T(8,128)S(1)}, u32[]{:S(2)}, u32[]{:S(2)}) collective-permute-start(f32[8,16384]{1,0:T(8,128)S(1)} %fusion.32), channel_id=1, source_target_pairs={{0,1},{1,0},{2,3},{3,2},{4,5},{5,4},{6,7},{7,6},{8,9},{9,8},{10,11... | collective-permute-start | bytes 1572872 | tf_op jit(solution)/shard_map/ppermute | solution.py:16
  224.8 8.8 %collective-permute-start.31 = (f32[8,1]{1,0:T(8,128)S(1)}, f32[8,1]{1,0:T(8,128)S(1)}, u32[]{:S(2)}, u32[]{:S(2)}) collective-permute-start(f32[8,1]{1,0:T(8,128)S(1)} %get-tuple-element.8), channel_id=1, source_target_pairs={{2,0},{4,2},{6,4},{8,6},{10,8},{12,10},{14,12},{16,14},{18,16},{20... | collective-permute-start | bytes 104 | tf_op jit(solution)/shard_map/ppermute | solution.py:27
  226.1 8.2 %collective-permute-start.30 = (f32[8,1]{1,0:T(8,128)S(1)}, f32[8,1]{1,0:T(8,128)S(1)}, u32[]{:S(2)}, u32[]{:S(2)}) collective-permute-start(f32[8,1]{1,0:T(8,128)S(1)} %get-tuple-element.7), channel_id=1, source_target_pairs={{0,2},{2,4},{4,6},{6,8},{8,10},{10,12},{12,14},{14,16},{16,18},{18... | collective-permute-start | bytes 104 | tf_op jit(solution)/shard_map/ppermute | solution.py:26
Sparse Core Ops, SparseCore 0:
  10.5 86.5 all-gather.1
  237.0 242.0 reduce-scatter.1
where the time goes:
time: 534 us; the launch traced here: 533 us
  waiting for transfers between devices  332 us (62%)
  starting transfers between devices  101 us (19%)
  blocking collectives  46.9 us (9%)
  local copies, waits for them, and re-layouts  14.9 us (3%)
  between operations  14 us (3%)
  other arithmetic  13.9 us (3%)
  matrix products  10.1 us (2%)
    reduce_scatter x1, waiting for transfers between devices, local(): lax.psum_scatter(jnp.zeros((inv_rows * lax.axis_size('mesh'), CELLS), jnp...  242 us
    all_gather x1, waiting for transfers between devices, local(): gathered = lax.all_gather(log_sigma, 'mesh', axis=0, tiled=True)  78.7 us
    ppermute x11, starting transfers between devices, with_halo(): before = lax.ppermute(last, axis, up)  63.6 us
    psum x1, blocking collectives, local(): return lax.psum(owned, ('group', 'comp'))  46.9 us
    ppermute x12, starting transfers between devices, from_partner(): return lax.ppermute(value, axis, pairs)  23.5 us
    ppermute x11, starting transfers between devices, with_halo(): after = lax.ppermute(initial, axis, down)  14.1 us
  transfers between devices with their start and end apart: 36, of which 12 were waited for; matrix products, arithmetic and copies ran while one was open for 2% of the time, Pallas kernels for 0%

commit v1 on v0

--- a/solution.py
+++ b/solution.py
@@ -63,7 +63,9 @@
     blocks_dev = owners.shape[0]
     inv_rows = log_sigma.shape[0]
     targets = owners * inv_rows + slots
-    gathered = lax.all_gather(log_sigma, "mesh", axis=0, tiled=True)
+    gathered = jnp.concatenate(
+        lax.all_to_all(jnp.stack([log_sigma] * lax.axis_size("mesh")), "mesh", 0, 0), axis=0
+    )
     model_part = jnp.take(gathered, targets, axis=0)
     sigmas = jnp.exp(model_part).reshape(-1)
     receivers = rcv_cell[0]

time: 534 us -> 484 us (0.906)
  waiting for transfers between devices: 332 us -> 267 us
  starting transfers between devices: 101 us -> 116 us
    all_gather x1 -> x0, waiting for transfers between devices: 78.7 us -> none  [local(): gathered = lax.all_gather(log_sigma, 'mesh', axis=0, tiled=True)]
    all_to_all x0 -> x1, waiting for transfers between devices: none -> 16.9 us  [local(): lax.all_to_all(jnp.stack([log_sigma] * lax.axis_size('mesh')), 'mesh', 0, 0)]
    all_to_all x0 -> x1, starting transfers between devices: none -> 13.2 us  [local(): lax.all_to_all(jnp.stack([log_sigma] * lax.axis_size('mesh')), 'mesh', 0, 0)]
where the time goes in v1:
time: 484 us; the launch traced here: 482 us
  waiting for transfers between devices  267 us (55%)
  starting transfers between devices  116 us (24%)
  blocking collectives  46.9 us (10%)
  local copies, waits for them, and re-layouts  15.5 us (3%)
  between operations  14 us (3%)
  other arithmetic  13.9 us (3%)
  matrix products  9.05 us (2%)
    reduce_scatter x1, waiting for transfers between devices, local(): lax.psum_scatter(jnp.zeros((inv_rows * lax.axis_size('mesh'), CELLS), jnp...  240 us
    ppermute x11, starting transfers between devices, with_halo(): before = lax.ppermute(last, axis, up)  64.8 us
    psum x1, blocking collectives, local(): return lax.psum(owned, ('group', 'comp'))  46.9 us
    ppermute x12, starting transfers between devices, from_partner(): return lax.ppermute(value, axis, pairs)  23.5 us
    all_to_all x1, waiting for transfers between devices, local(): lax.all_to_all(jnp.stack([log_sigma] * lax.axis_size('mesh')), 'mesh', 0, 0)  16.9 us
    ppermute x11, starting transfers between devices, with_halo(): after = lax.ppermute(initial, axis, down)  14.1 us
    all_to_all x1, starting transfers between devices, local(): lax.all_to_all(jnp.stack([log_sigma] * lax.axis_size('mesh')), 'mesh', 0, 0)  13.2 us
    ppermute x11, waiting for transfers between devices, with_halo(): before = lax.ppermute(last, axis, up)  10.1 us
  transfers between devices with their start and end apart: 36, of which 12 were waited for; matrix products, arithmetic and copies ran while one was open for 2% of the time, Pallas kernels for 0%

profile of v1, /device:TPU:32, one launch (start us, length us, event | category | flops | bytes accessed | tf_op | source)
XLA Modules:
  0.0 482.2 jit_solution(8464868465338218760)
XLA Ops:
  6.5 1.9 stack.2
  8.5 13.2 %all-to-all-start = ((f32[32,64,128]{2,1,0:T(8,128)}), f32[32,64,128]{2,1,0:T(8,128)S(1)}, u32[]{:S(2)}, u32[]{:S(2)}) async-start(f32[32,64,128]{2,1,0:T(8,128)} %stack.2), calls=%async_computation | async-start | bytes 2097152 | tf_op jit(solution)/shard_map/all_to_all | solution.py:67
  21.7 1.3 collective-permute-start.1
  23.0 4.5 collective-permute-start
  27.6 1.9 collective-permute-start.2
  32.8 16.9 %all-to-all-done = f32[32,64,128]{2,1,0:T(8,128)S(1)} async-done(((f32[32,64,128]{2,1,0:T(8,128)}), f32[32,64,128]{2,1,0:T(8,128)S(1)}, u32[]{:S(2)}, u32[]{:S(2)}) %all-to-all-start) | async-done | bytes 1048608 | tf_op jit(solution)/shard_map/all_to_all | solution.py:67
  50.5 1.7 fusion.8
  52.1 1.9 collective-permute-start.5
  54.1 1.3 collective-permute-start.4
  55.4 4.5 collective-permute-start.3
  60.0 1.3 collective-permute-done.3
  62.2 1.9 collective-permute-start.8
  64.2 1.3 collective-permute-start.7
  65.5 4.8 collective-permute-start.6
  72.1 1.9 collective-permute-start.11
  74.1 1.3 collective-permute-start.10
  75.4 4.8 collective-permute-start.9
  80.2 1.3 collective-permute-done.9
  82.5 1.9 collective-permute-start.14
  84.5 1.3 collective-permute-start.13
  85.7 4.8 collective-permute-start.12
  92.4 1.9 collective-permute-start.17
  95.1 1.3 collective-permute-start.16
  96.4 6.7 %collective-permute-start.15 = (f32[8,1]{1,0:T(8,128)S(1)}, f32[8,1]{1,0:T(8,128)S(1)}, u32[]{:S(2)}, u32[]{:S(2)}) collective-permute-start(f32[8,1]{1,0:T(8,128)S(1)} %get-tuple-element.17), channel_id=1, source_target_pairs={{0,2},{2,4},{4,6},{6,8},{8,10},{10,12},{12,14},{14,16},{16,18},{18... | collective-permute-start | bytes 104 | tf_op jit(solution)/shard_map/ppermute | solution.py:26
  103.1 1.3 collective-permute-done.15
  104.4 1.9 fusion.18
  106.3 5.3 %copy.271 = f32[8,16384]{0,1:T(8,128)} copy(f32[8,16384]{1,0:T(8,128)S(1)} %fusion.18) | data formatting | bytes 1048576 | tf_op jit(solution)/shard_map/add | solution.py:56
  111.6 6.0 %scatter_custom_fusion = f32[8,16384]{0,1:T(8,128)} fusion(s32[128]{0:T(128)S(1)} %fusion.122, f32[]{:T(128)} %constant.12.clone.1, f32[1,1,8,128]{2,3,1,0:T(8,128)S(1)} %copy.272, f32[8,16384]{0,1:T(8,128)} %copy.271, s32[1024]{0:T(1024)S(1)} %pad_clamp_fusion), kind=kCustom, calls=%fused_computation.15 | custom fusion | flops 2048 | bytes 1118212 | tf_op jit(solution)/shard_map/scatter-add | solution.py:79
  117.6 5.5 %copy.273 = f32[8,16384]{1,0:T(8,128)S(1)} copy(f32[8,16384]{0,1:T(8,128)} %scatter_custom_fusion) | data formatting | bytes 1048576 | tf_op jit(solution)/shard_map/scatter-add | solution.py:79
  123.6 1.9 collective-permute-start.20
  126.8 6.9 %collective-permute-start.18 = (f32[8,1]{1,0:T(8,128)S(1)}, f32[8,1]{1,0:T(8,128)S(1)}, u32[]{:S(2)}, u32[]{:S(2)}) collective-permute-start(f32[8,1]{1,0:T(8,128)S(1)} %get-tuple-element.15), channel_id=1, source_target_pairs={{0,2},{2,4},{4,6},{6,8},{8,10},{10,12},{12,14},{14,16},{16,18},{18... | collective-permute-start | bytes 104 | tf_op jit(solution)/shard_map/ppermute | solution.py:26
  133.8 1.3 collective-permute-done.18
  135.7 1.9 collective-permute-start.23
  137.7 1.3 collective-permute-start.22
  139.0 6.9 %collective-permute-start.21 = (f32[8,1]{1,0:T(8,128)S(1)}, f32[8,1]{1,0:T(8,128)S(1)}, u32[]{:S(2)}, u32[]{:S(2)}) collective-permute-start(f32[8,1]{1,0:T(8,128)S(1)} %get-tuple-element.13), channel_id=1, source_target_pairs={{0,2},{2,4},{4,6},{6,8},{8,10},{10,12},{12,14},{14,16},{16,18},{18... | collective-permute-start | bytes 104 | tf_op jit(solution)/shard_map/ppermute | solution.py:26
  147.7 1.9 collective-permute-start.26
  149.7 1.3 collective-permute-start.25
  151.0 6.9 %collective-permute-start.24 = (f32[8,1]{1,0:T(8,128)S(1)}, f32[8,1]{1,0:T(8,128)S(1)}, u32[]{:S(2)}, u32[]{:S(2)}) collective-permute-start(f32[8,1]{1,0:T(8,128)S(1)} %get-tuple-element.11), channel_id=1, source_target_pairs={{0,2},{2,4},{4,6},{6,8},{8,10},{10,12},{12,14},{14,16},{16,18},{18... | collective-permute-start | bytes 104 | tf_op jit(solution)/shard_map/ppermute | solution.py:26
  157.9 1.3 collective-permute-done.24
  159.9 1.9 collective-permute-start.29
  161.8 2.4 collective-permute-start.33
  165.6 6.9 %collective-permute-start.27 = (f32[8,1]{1,0:T(8,128)S(1)}, f32[8,1]{1,0:T(8,128)S(1)}, u32[]{:S(2)}, u32[]{:S(2)}) collective-permute-start(f32[8,1]{1,0:T(8,128)S(1)} %get-tuple-element.9), channel_id=1, source_target_pairs={{0,2},{2,4},{4,6},{6,8},{8,10},{10,12},{12,14},{14,16},{16,18},{18... | collective-permute-start | bytes 104 | tf_op jit(solution)/shard_map/ppermute | solution.py:26
  174.3 1.9 collective-permute-start.32
  176.3 1.3 collective-permute-start.31
  177.6 6.9 %collective-permute-start.30 = (f32[8,1]{1,0:T(8,128)S(1)}, f32[8,1]{1,0:T(8,128)S(1)}, u32[]{:S(2)}, u32[]{:S(2)}) collective-permute-start(f32[8,1]{1,0:T(8,128)S(1)} %get-tuple-element.7), channel_id=1, source_target_pairs={{0,2},{2,4},{4,6},{6,8},{8,10},{10,12},{12,14},{14,16},{16,18},{18... | collective-permute-start | bytes 104 | tf_op jit(solution)/shard_map/ppermute | solution.py:26
  186.2 2.1 scatter_custom_fusion.1
  188.3 240.1 %reduce-scatter.2.cloned.1.call-done = f32[64,128]{1,0:T(8,128)} async-done(((f32[2048,128]{1,0:T(8,128)}), f32[64,128]{1,0:T(8,128)}) %reduce-scatter.2.cloned.1.call-update) | async-done | bytes 32784 | tf_op jit(solution)/shard_map/reduce_scatter | solution.py:85
  428.4 46.9 %psum.7 = f32[64,128]{1,0:T(8,128)} all-reduce(f32[64,128]{1,0:T(8,128)} %reduce-scatter.2.cloned.1.call-done), channel_id=1, replica_groups=mesh['group'=8,'mesh'=32,'comp'=2] {'group','comp'}, use_global_device_ids=true, to_apply=%region_4.5 | all-reduce | flops 8192 | bytes 65536 | tf_op jit(solution)/shard_map/psum | solution.py:93
  (82 shorter events, 20.3 us)
Async XLA Ops:
  6.5 23.0 %copy-start = (f32[128,128]{1,0:T(8,128)S(1)}, f32[128,128]{1,0:T(8,128)}, u32[]{:S(2)}) copy-start(f32[128,128]{1,0:T(8,128)} %param.10) | copy-start | bytes 196612
  6.5 54.8 %copy-start.1 = (f32[1,1,8,128,128]{4,3,2,1,0:T(8,128)S(1)}, f32[1,1,8,128,128]{4,3,2,1,0:T(8,128)}, u32[]{:S(2)}) copy-start(f32[1,1,8,128,128]{4,3,2,1,0:T(8,128)} %param.11) | copy-start | bytes 1572868
  8.5 41.2 %all-to-all-start = ((f32[32,64,128]{2,1,0:T(8,128)}), f32[32,64,128]{2,1,0:T(8,128)S(1)}, u32[]{:S(2)}, u32[]{:S(2)}) async-start(f32[32,64,128]{2,1,0:T(8,128)} %stack.2), calls=%async_computation | async-start | bytes 2097152 | tf_op jit(solution)/shard_map/all_to_all | solution.py:67
  21.6 406.8 %reduce-scatter.2.cloned.1.call-start = ((), (), s32[]{:S(2)}) async-start(), calls=%async_computation.2 | async-start | bytes 1081344 | tf_op jit(solution)/shard_map/reduce_scatter | solution.py:85
  21.7 28.8 %collective-permute-start.1 = (f32[8,1]{1,0:T(8,128)S(1)}, f32[8,1]{1,0:T(8,128)S(1)}, u32[]{:S(2)}, u32[]{:S(2)}) collective-permute-start(f32[8,1]{1,0:T(8,128)S(1)} %broadcast.159), channel_id=1, source_target_pairs={{2,0},{4,2},{6,4},{8,6},{10,8},{12,10},{14,12},{16,14},{18,16},{20... | collective-permute-start | bytes 104 | tf_op jit(solution)/shard_map/ppermute | solution.py:27
  23.0 27.5 %collective-permute-start = (f32[8,1]{1,0:T(8,128)S(1)}, f32[8,1]{1,0:T(8,128)S(1)}, u32[]{:S(2)}, u32[]{:S(2)}) collective-permute-start(f32[8,1]{1,0:T(8,128)S(1)} %broadcast.159), channel_id=1, source_target_pairs={{0,2},{2,4},{4,6},{6,8},{8,10},{10,12},{12,14},{14,16},{16,18},{18... | collective-permute-start | bytes 104 | tf_op jit(solution)/shard_map/ppermute | solution.py:26
  27.6 66.7 %copy-start.3 = (s32[1,128]{1,0:T(1,128)S(1)}, s32[1,128]{1,0:T(1,128)}, u32[]{:S(2)}) copy-start(s32[1,128]{1,0:T(1,128)} %param.12) | copy-start | bytes 1540
  27.6 66.7 %copy-start.2 = (f32[1,1,8,128]{3,2,1,0:T(8,128)S(1)}, f32[1,1,8,128]{3,2,1,0:T(8,128)}, u32[]{:S(2)}) copy-start(f32[1,1,8,128]{3,2,1,0:T(8,128)} %param.13) | copy-start | bytes 12292
  27.6 22.9 %collective-permute-start.2 = (f32[8,16384]{1,0:T(8,128)S(1)}, f32[8,16384]{1,0:T(8,128)S(1)}, u32[]{:S(2)}, u32[]{:S(2)}) collective-permute-start(f32[8,16384]{1,0:T(8,128)S(1)} %broadcast.156.clone), channel_id=1, source_target_pairs={{0,1},{1,0},{2,3},{3,2},{4,5},{5,4},{6,7},{7,6},{8,9},{9,8},{10,11... | collective-permute-start | bytes 1572872 | tf_op jit(solution)/shard_map/ppermute | solution.py:16
  52.1 9.2 %collective-permute-start.5 = (f32[8,16384]{1,0:T(8,128)S(1)}, f32[8,16384]{1,0:T(8,128)S(1)}, u32[]{:S(2)}, u32[]{:S(2)}) collective-permute-start(f32[8,16384]{1,0:T(8,128)S(1)} %fusion.8), channel_id=1, source_target_pairs={{0,1},{1,0},{2,3},{3,2},{4,5},{5,4},{6,7},{7,6},{8,9},{9,8},{10,11... | collective-permute-start | bytes 1572872 | tf_op jit(solution)/shard_map/ppermute | solution.py:16
  54.1 5.8 %collective-permute-start.4 = (f32[8,1]{1,0:T(8,128)S(1)}, f32[8,1]{1,0:T(8,128)S(1)}, u32[]{:S(2)}, u32[]{:S(2)}) collective-permute-start(f32[8,1]{1,0:T(8,128)S(1)} %get-tuple-element.26), channel_id=1, source_target_pairs={{2,0},{4,2},{6,4},{8,6},{10,8},{12,10},{14,12},{16,14},{18,16},{20... | collective-permute-start | bytes 104 | tf_op jit(solution)/shard_map/ppermute | solution.py:27
  55.4 5.9 %collective-permute-start.3 = (f32[8,1]{1,0:T(8,128)S(1)}, f32[8,1]{1,0:T(8,128)S(1)}, u32[]{:S(2)}, u32[]{:S(2)}) collective-permute-start(f32[8,1]{1,0:T(8,128)S(1)} %get-tuple-element.25), channel_id=1, source_target_pairs={{0,2},{2,4},{4,6},{6,8},{8,10},{10,12},{12,14},{14,16},{16,18},{18... | collective-permute-start | bytes 104 | tf_op jit(solution)/shard_map/ppermute | solution.py:26
  62.2 9.4 %collective-permute-start.8 = (f32[8,16384]{1,0:T(8,128)S(1)}, f32[8,16384]{1,0:T(8,128)S(1)}, u32[]{:S(2)}, u32[]{:S(2)}) collective-permute-start(f32[8,16384]{1,0:T(8,128)S(1)} %fusion.10), channel_id=1, source_target_pairs={{0,1},{1,0},{2,3},{3,2},{4,5},{5,4},{6,7},{7,6},{8,9},{9,8},{10,11... | collective-permute-start | bytes 1572872 | tf_op jit(solution)/shard_map/ppermute | solution.py:16
  64.2 6.7 %collective-permute-start.7 = (f32[8,1]{1,0:T(8,128)S(1)}, f32[8,1]{1,0:T(8,128)S(1)}, u32[]{:S(2)}, u32[]{:S(2)}) collective-permute-start(f32[8,1]{1,0:T(8,128)S(1)} %get-tuple-element.24), channel_id=1, source_target_pairs={{2,0},{4,2},{6,4},{8,6},{10,8},{12,10},{14,12},{16,14},{18,16},{20... | collective-permute-start | bytes 104 | tf_op jit(solution)/shard_map/ppermute | solution.py:27
  65.5 6.1 %collective-permute-start.6 = (f32[8,1]{1,0:T(8,128)S(1)}, f32[8,1]{1,0:T(8,128)S(1)}, u32[]{:S(2)}, u32[]{:S(2)}) collective-permute-start(f32[8,1]{1,0:T(8,128)S(1)} %get-tuple-element.23), channel_id=1, source_target_pairs={{0,2},{2,4},{4,6},{6,8},{8,10},{10,12},{12,14},{14,16},{16,18},{18... | collective-permute-start | bytes 104 | tf_op jit(solution)/shard_map/ppermute | solution.py:26
  72.1 9.4 %collective-permute-start.11 = (f32[8,16384]{1,0:T(8,128)S(1)}, f32[8,16384]{1,0:T(8,128)S(1)}, u32[]{:S(2)}, u32[]{:S(2)}) collective-permute-start(f32[8,16384]{1,0:T(8,128)S(1)} %fusion.12), channel_id=1, source_target_pairs={{0,1},{1,0},{2,3},{3,2},{4,5},{5,4},{6,7},{7,6},{8,9},{9,8},{10,11... | collective-permute-start | bytes 1572872 | tf_op jit(solution)/shard_map/ppermute | solution.py:16
  74.1 6.1 %collective-permute-start.10 = (f32[8,1]{1,0:T(8,128)S(1)}, f32[8,1]{1,0:T(8,128)S(1)}, u32[]{:S(2)}, u32[]{:S(2)}) collective-permute-start(f32[8,1]{1,0:T(8,128)S(1)} %get-tuple-element.22), channel_id=1, source_target_pairs={{2,0},{4,2},{6,4},{8,6},{10,8},{12,10},{14,12},{16,14},{18,16},{20... | collective-permute-start | bytes 104 | tf_op jit(solution)/shard_map/ppermute | solution.py:27
  75.4 6.1 %collective-permute-start.9 = (f32[8,1]{1,0:T(8,128)S(1)}, f32[8,1]{1,0:T(8,128)S(1)}, u32[]{:S(2)}, u32[]{:S(2)}) collective-permute-start(f32[8,1]{1,0:T(8,128)S(1)} %get-tuple-element.21), channel_id=1, source_target_pairs={{0,2},{2,4},{4,6},{6,8},{8,10},{10,12},{12,14},{14,16},{16,18},{18... | collective-permute-start | bytes 104 | tf_op jit(solution)/shard_map/ppermute | solution.py:26
  82.5 9.4 %collective-permute-start.14 = (f32[8,16384]{1,0:T(8,128)S(1)}, f32[8,16384]{1,0:T(8,128)S(1)}, u32[]{:S(2)}, u32[]{:S(2)}) collective-permute-start(f32[8,16384]{1,0:T(8,128)S(1)} %fusion.14), channel_id=1, source_target_pairs={{0,1},{1,0},{2,3},{3,2},{4,5},{5,4},{6,7},{7,6},{8,9},{9,8},{10,11... | collective-permute-start | bytes 1572872 | tf_op jit(solution)/shard_map/ppermute | solution.py:16
  84.5 6.7 %collective-permute-start.13 = (f32[8,1]{1,0:T(8,128)S(1)}, f32[8,1]{1,0:T(8,128)S(1)}, u32[]{:S(2)}, u32[]{:S(2)}) collective-permute-start(f32[8,1]{1,0:T(8,128)S(1)} %get-tuple-element.20), channel_id=1, source_target_pairs={{2,0},{4,2},{6,4},{8,6},{10,8},{12,10},{14,12},{16,14},{18,16},{20... | collective-permute-start | bytes 104 | tf_op jit(solution)/shard_map/ppermute | solution.py:27
  85.7 6.1 %collective-permute-start.12 = (f32[8,1]{1,0:T(8,128)S(1)}, f32[8,1]{1,0:T(8,128)S(1)}, u32[]{:S(2)}, u32[]{:S(2)}) collective-permute-start(f32[8,1]{1,0:T(8,128)S(1)} %get-tuple-element.19), channel_id=1, source_target_pairs={{0,2},{2,4},{4,6},{6,8},{8,10},{10,12},{12,14},{14,16},{16,18},{18... | collective-permute-start | bytes 104 | tf_op jit(solution)/shard_map/ppermute | solution.py:26
  92.4 12.0 %collective-permute-start.17 = (f32[8,16384]{1,0:T(8,128)S(1)}, f32[8,16384]{1,0:T(8,128)}, u32[]{:S(2)}, u32[]{:S(2)}) collective-permute-start(f32[8,16384]{1,0:T(8,128)S(1)} %fusion.16), channel_id=1, source_target_pairs={{0,1},{1,0},{2,3},{3,2},{4,5},{5,4},{6,7},{7,6},{8,9},{9,8},{10,11... | collective-permute-start | bytes 1572872 | tf_op jit(solution)/shard_map/ppermute | solution.py:16
  95.1 8.0 %collective-permute-start.16 = (f32[8,1]{1,0:T(8,128)S(1)}, f32[8,1]{1,0:T(8,128)S(1)}, u32[]{:S(2)}, u32[]{:S(2)}) collective-permute-start(f32[8,1]{1,0:T(8,128)S(1)} %get-tuple-element.18), channel_id=1, source_target_pairs={{2,0},{4,2},{6,4},{8,6},{10,8},{12,10},{14,12},{16,14},{18,16},{20... | collective-permute-start | bytes 104 | tf_op jit(solution)/shard_map/ppermute | solution.py:27
  96.4 8.0 %collective-permute-start.15 = (f32[8,1]{1,0:T(8,128)S(1)}, f32[8,1]{1,0:T(8,128)S(1)}, u32[]{:S(2)}, u32[]{:S(2)}) collective-permute-start(f32[8,1]{1,0:T(8,128)S(1)} %get-tuple-element.17), channel_id=1, source_target_pairs={{0,2},{2,4},{4,6},{6,8},{8,10},{10,12},{12,14},{14,16},{16,18},{18... | collective-permute-start | bytes 104 | tf_op jit(solution)/shard_map/ppermute | solution.py:26
  123.6 11.5 %collective-permute-start.20 = (f32[8,16384]{1,0:T(8,128)S(1)}, f32[8,16384]{1,0:T(8,128)S(1)}, u32[]{:S(2)}, u32[]{:S(2)}) collective-permute-start(f32[8,16384]{1,0:T(8,128)S(1)} %fusion.5), channel_id=1, source_target_pairs={{0,1},{1,0},{2,3},{3,2},{4,5},{5,4},{6,7},{7,6},{8,9},{9,8},{10,11... | collective-permute-start | bytes 1572872 | tf_op jit(solution)/shard_map/ppermute | solution.py:16
  125.6 8.2 %collective-permute-start.19 = (f32[8,1]{1,0:T(8,128)S(1)}, f32[8,1]{1,0:T(8,128)S(1)}, u32[]{:S(2)}, u32[]{:S(2)}) collective-permute-start(f32[8,1]{1,0:T(8,128)S(1)} %get-tuple-element.16), channel_id=1, source_target_pairs={{2,0},{4,2},{6,4},{8,6},{10,8},{12,10},{14,12},{16,14},{18,16},{20... | collective-permute-start | bytes 104 | tf_op jit(solution)/shard_map/ppermute | solution.py:27
  126.8 8.2 %collective-permute-start.18 = (f32[8,1]{1,0:T(8,128)S(1)}, f32[8,1]{1,0:T(8,128)S(1)}, u32[]{:S(2)}, u32[]{:S(2)}) collective-permute-start(f32[8,1]{1,0:T(8,128)S(1)} %get-tuple-element.15), channel_id=1, source_target_pairs={{0,2},{2,4},{4,6},{6,8},{8,10},{10,12},{12,14},{14,16},{16,18},{18... | collective-permute-start | bytes 104 | tf_op jit(solution)/shard_map/ppermute | solution.py:26
  135.7 11.6 %collective-permute-start.23 = (f32[8,16384]{1,0:T(8,128)S(1)}, f32[8,16384]{1,0:T(8,128)S(1)}, u32[]{:S(2)}, u32[]{:S(2)}) collective-permute-start(f32[8,16384]{1,0:T(8,128)S(1)} %fusion.50), channel_id=1, source_target_pairs={{0,1},{1,0},{2,3},{3,2},{4,5},{5,4},{6,7},{7,6},{8,9},{9,8},{10,11... | collective-permute-start | bytes 1572872 | tf_op jit(solution)/shard_map/ppermute | solution.py:16
  137.7 8.8 %collective-permute-start.22 = (f32[8,1]{1,0:T(8,128)S(1)}, f32[8,1]{1,0:T(8,128)S(1)}, u32[]{:S(2)}, u32[]{:S(2)}) collective-permute-start(f32[8,1]{1,0:T(8,128)S(1)} %get-tuple-element.14), channel_id=1, source_target_pairs={{2,0},{4,2},{6,4},{8,6},{10,8},{12,10},{14,12},{16,14},{18,16},{20... | collective-permute-start | bytes 104 | tf_op jit(solution)/shard_map/ppermute | solution.py:27
  139.0 8.3 %collective-permute-start.21 = (f32[8,1]{1,0:T(8,128)S(1)}, f32[8,1]{1,0:T(8,128)S(1)}, u32[]{:S(2)}, u32[]{:S(2)}) collective-permute-start(f32[8,1]{1,0:T(8,128)S(1)} %get-tuple-element.13), channel_id=1, source_target_pairs={{0,2},{2,4},{4,6},{6,8},{8,10},{10,12},{12,14},{14,16},{16,18},{18... | collective-permute-start | bytes 104 | tf_op jit(solution)/shard_map/ppermute | solution.py:26
  147.7 11.5 %collective-permute-start.26 = (f32[8,16384]{1,0:T(8,128)S(1)}, f32[8,16384]{1,0:T(8,128)S(1)}, u32[]{:S(2)}, u32[]{:S(2)}) collective-permute-start(f32[8,16384]{1,0:T(8,128)S(1)} %fusion.44), channel_id=1, source_target_pairs={{0,1},{1,0},{2,3},{3,2},{4,5},{5,4},{6,7},{7,6},{8,9},{9,8},{10,11... | collective-permute-start | bytes 1572872 | tf_op jit(solution)/shard_map/ppermute | solution.py:16
  149.7 8.2 %collective-permute-start.25 = (f32[8,1]{1,0:T(8,128)S(1)}, f32[8,1]{1,0:T(8,128)S(1)}, u32[]{:S(2)}, u32[]{:S(2)}) collective-permute-start(f32[8,1]{1,0:T(8,128)S(1)} %get-tuple-element.12), channel_id=1, source_target_pairs={{2,0},{4,2},{6,4},{8,6},{10,8},{12,10},{14,12},{16,14},{18,16},{20... | collective-permute-start | bytes 104 | tf_op jit(solution)/shard_map/ppermute | solution.py:27
  151.0 8.2 %collective-permute-start.24 = (f32[8,1]{1,0:T(8,128)S(1)}, f32[8,1]{1,0:T(8,128)S(1)}, u32[]{:S(2)}, u32[]{:S(2)}) collective-permute-start(f32[8,1]{1,0:T(8,128)S(1)} %get-tuple-element.11), channel_id=1, source_target_pairs={{0,2},{2,4},{4,6},{6,8},{8,10},{10,12},{12,14},{14,16},{16,18},{18... | collective-permute-start | bytes 104 | tf_op jit(solution)/shard_map/ppermute | solution.py:26
  159.9 14.0 %collective-permute-start.29 = (f32[8,16384]{1,0:T(8,128)S(1)}, f32[8,16384]{1,0:T(8,128)S(1)}, u32[]{:S(2)}, u32[]{:S(2)}) collective-permute-start(f32[8,16384]{1,0:T(8,128)S(1)} %fusion.38), channel_id=1, source_target_pairs={{0,1},{1,0},{2,3},{3,2},{4,5},{5,4},{6,7},{7,6},{8,9},{9,8},{10,11... | collective-permute-start | bytes 1572872 | tf_op jit(solution)/shard_map/ppermute | solution.py:16
  161.8 23.2 %collective-permute-start.33 = (f32[8,16384]{1,0:T(8,128)S(1)}, f32[8,16384]{1,0:T(8,128)S(1)}, u32[]{:S(2)}, u32[]{:S(2)}) collective-permute-start(f32[8,16384]{1,0:T(8,128)S(1)} %fusion.18), channel_id=1, source_target_pairs={{0,1},{1,0},{2,3},{3,2},{4,5},{5,4},{6,7},{7,6},{8,9},{9,8},{10,11... | collective-permute-start | bytes 1572872 | tf_op jit(solution)/shard_map/ppermute | solution.py:16
  164.3 8.8 %collective-permute-start.28 = (f32[8,1]{1,0:T(8,128)S(1)}, f32[8,1]{1,0:T(8,128)S(1)}, u32[]{:S(2)}, u32[]{:S(2)}) collective-permute-start(f32[8,1]{1,0:T(8,128)S(1)} %get-tuple-element.10), channel_id=1, source_target_pairs={{2,0},{4,2},{6,4},{8,6},{10,8},{12,10},{14,12},{16,14},{18,16},{20... | collective-permute-start | bytes 104 | tf_op jit(solution)/shard_map/ppermute | solution.py:27
  165.6 8.2 %collective-permute-start.27 = (f32[8,1]{1,0:T(8,128)S(1)}, f32[8,1]{1,0:T(8,128)S(1)}, u32[]{:S(2)}, u32[]{:S(2)}) collective-permute-start(f32[8,1]{1,0:T(8,128)S(1)} %get-tuple-element.9), channel_id=1, source_target_pairs={{0,2},{2,4},{4,6},{6,8},{8,10},{10,12},{12,14},{14,16},{16,18},{18... | collective-permute-start | bytes 104 | tf_op jit(solution)/shard_map/ppermute | solution.py:26
  174.3 11.5 %collective-permute-start.32 = (f32[8,16384]{1,0:T(8,128)S(1)}, f32[8,16384]{1,0:T(8,128)S(1)}, u32[]{:S(2)}, u32[]{:S(2)}) collective-permute-start(f32[8,16384]{1,0:T(8,128)S(1)} %fusion.32), channel_id=1, source_target_pairs={{0,1},{1,0},{2,3},{3,2},{4,5},{5,4},{6,7},{7,6},{8,9},{9,8},{10,11... | collective-permute-start | bytes 1572872 | tf_op jit(solution)/shard_map/ppermute | solution.py:16
  176.3 8.8 %collective-permute-start.31 = (f32[8,1]{1,0:T(8,128)S(1)}, f32[8,1]{1,0:T(8,128)S(1)}, u32[]{:S(2)}, u32[]{:S(2)}) collective-permute-start(f32[8,1]{1,0:T(8,128)S(1)} %get-tuple-element.8), channel_id=1, source_target_pairs={{2,0},{4,2},{6,4},{8,6},{10,8},{12,10},{14,12},{16,14},{18,16},{20... | collective-permute-start | bytes 104 | tf_op jit(solution)/shard_map/ppermute | solution.py:27
  177.6 8.2 %collective-permute-start.30 = (f32[8,1]{1,0:T(8,128)S(1)}, f32[8,1]{1,0:T(8,128)S(1)}, u32[]{:S(2)}, u32[]{:S(2)}) collective-permute-start(f32[8,1]{1,0:T(8,128)S(1)} %get-tuple-element.7), channel_id=1, source_target_pairs={{0,2},{2,4},{4,6},{6,8},{8,10},{10,12},{12,14},{14,16},{16,18},{18... | collective-permute-start | bytes 104 | tf_op jit(solution)/shard_map/ppermute | solution.py:26
Sparse Core Ops, SparseCore 0:
  188.5 239.9 reduce-scatter.1
